TPU v7x, 32 devices: a whole 2x2x4 slice. The times are simulated.
32 devices in a mesh: dp: 8 (over z, y), seq: 4 (over x, core).
Axes of the slice: x: 2, y: 2, z: 4, core: 2. Of those that a mesh axis runs over, the one named last changes fastest.
Arguments:
- inputs: bfloat16 [16, 1024, 768], P('dp', 'seq'), may hold values from -6 to 6
- lengths: int32 [16], P('dp'), may hold values from 512 to 1024, as said below
- query_weight: bfloat16 [768, 768], P('dp'), may hold values from -0.3125 to 0.3125
- key_weight: bfloat16 [768, 768], P('dp'), may hold values from -0.3125 to 0.3125
- value_weight: bfloat16 [768, 768], P('dp'), may hold values from -0.21875 to 0.21875
- output_weight: bfloat16 [768, 768], P('dp'), may hold values from -0.625 to 0.625
- up_weight: bfloat16 [768, 3072], P('dp'), may hold values from -0.21875 to 0.21875
- down_weight: bfloat16 [3072, 768], P('dp'), may hold values from -0.15625 to 0.15625
- query_bias: bfloat16 [768], P('dp'), may hold values from -3 to 3
- value_bias: bfloat16 [768], P('dp'), may hold values from -3 to 3
- output_bias: bfloat16 [768], P('dp'), may hold values from -3 to 3
- up_bias: bfloat16 [3072], P('dp'), may hold values from -3 to 3
- down_bias: bfloat16 [768], P('dp'), may hold values from -3 to 3
- first_gain: bfloat16 [768], P('dp'), may hold values from 0.5 to 1.5
- first_shift: bfloat16 [768], P('dp'), may hold values from -2 to 2
- second_gain: bfloat16 [768], P('dp'), may hold values from 0.5 to 1.5
- second_shift: bfloat16 [768], P('dp'), may hold values from -2 to 2
- cotangent: bfloat16 [16, 1024, 768], P('dp', 'seq'), may hold values from -6 to 6
Outputs:
- layer_out: bfloat16 [16, 1024, 768], P('dp', 'seq')
- input_grad: bfloat16 [16, 1024, 768], P('dp', 'seq')
- query_weight_grad: float32 [768, 768], P('dp')
- key_weight_grad: float32 [768, 768], P('dp')
- value_weight_grad: float32 [768, 768], P('dp')
- output_weight_grad: float32 [768, 768], P('dp')
- up_weight_grad: float32 [768, 3072], P('dp')
- down_weight_grad: float32 [3072, 768], P('dp')
- query_bias_grad: float32 [768], P('dp')
- value_bias_grad: float32 [768], P('dp')
- output_bias_grad: float32 [768], P('dp')
- up_bias_grad: float32 [3072], P('dp')
- down_bias_grad: float32 [768], P('dp')
- first_gain_grad: float32 [768], P('dp')
- first_shift_grad: float32 [768], P('dp')
- second_gain_grad: float32 [768], P('dp')
- second_shift_grad: float32 [768], P('dp')
Inputs may be any that keep to these rules, and one draw needn't show every extreme that they name: `lengths`: the number of real tokens of each sequence; its later positions up to 1024 are padding.
All inputs are finite; a program needn't handle non-finite values.
Results may differ from a plain program's by a relative error of at most 0.015.
Values may be sent and summed in bfloat16 or wider, within the bound.
A program may use at most 192 MiB of HBM per device.

v0:
```python
import jax
import jax.numpy as jnp
from jax import lax
from jax.sharding import PartitionSpec as P

HEAD_DIM = 64


eps_norm = 1e-05
masked_score = -1000000000.0


def layer_norm(hidden, gain_vec, shift_vec):
    row_mean = jnp.mean(hidden, axis=-1, keepdims=True)
    centred = hidden - row_mean
    row_var = jnp.mean(centred * centred, axis=-1, keepdims=True)
    return centred * lax.rsqrt(row_var + eps_norm) * gain_vec + shift_vec


def gelu_exact(pre_act):
    return jax.nn.gelu(pre_act, approximate=False)


def matmul_plain(first_op, second_op):
    return jnp.dot(first_op, second_op, preferred_element_type=jnp.float32)


def inner_rows(first_op, second_op):
    return lax.dot_general(
        first_op, second_op, (((0,), (0,)), ((), ())), preferred_element_type=jnp.float32
    )


def times_transposed(first_op, second_op):
    return lax.dot_general(
        first_op, second_op, (((1,), (1,)), ((), ())), preferred_element_type=jnp.float32
    )


def column_sums(grad_rows):
    return jnp.sum(grad_rows.astype(jnp.float32), axis=0)


def local(
    inputs,
    lengths,
    query_weight,
    key_weight,
    value_weight,
    output_weight,
    up_weight,
    down_weight,
    query_bias,
    value_bias,
    output_bias,
    up_bias,
    down_bias,
    first_gain,
    first_shift,
    second_gain,
    second_shift,
    cotangent,
):
    gathered = (
        lax.all_gather(query_weight, "dp", axis=0, tiled=True),
        lax.all_gather(key_weight, "dp", axis=0, tiled=True),
        lax.all_gather(value_weight, "dp", axis=0, tiled=True),
        lax.all_gather(output_weight, "dp", axis=0, tiled=True),
        lax.all_gather(up_weight, "dp", axis=0, tiled=True),
        lax.all_gather(down_weight, "dp", axis=0, tiled=True),
        lax.all_gather(query_bias, "dp", axis=0, tiled=True),
        lax.all_gather(value_bias, "dp", axis=0, tiled=True),
        lax.all_gather(output_bias, "dp", axis=0, tiled=True),
        lax.all_gather(up_bias, "dp", axis=0, tiled=True),
        lax.all_gather(down_bias, "dp", axis=0, tiled=True),
        lax.all_gather(first_gain, "dp", axis=0, tiled=True),
        lax.all_gather(first_shift, "dp", axis=0, tiled=True),
        lax.all_gather(second_gain, "dp", axis=0, tiled=True),
        lax.all_gather(second_shift, "dp", axis=0, tiled=True),
    )
    full_query, full_key, full_value, full_output, full_up, full_down = gathered[0:6]
    bias_query = gathered[6].astype(jnp.float32)
    bias_value = gathered[7].astype(jnp.float32)
    bias_output = gathered[8].astype(jnp.float32)
    bias_up = gathered[9].astype(jnp.float32)
    bias_down = gathered[10].astype(jnp.float32)
    gain_first = gathered[11].astype(jnp.float32)
    shift_first = gathered[12].astype(jnp.float32)
    gain_second = gathered[13].astype(jnp.float32)
    shift_second = gathered[14].astype(jnp.float32)
    group_count, local_len, model_width = inputs.shape
    row_count = group_count * local_len
    flat_in = inputs.reshape(row_count, model_width)
    queries = (matmul_plain(flat_in, full_query) + bias_query).astype(jnp.bfloat16)
    key_rows = matmul_plain(flat_in, full_key).astype(jnp.bfloat16)
    value_rows = (matmul_plain(flat_in, full_value) + bias_value).astype(jnp.bfloat16)
    stacked = jnp.stack([queries, key_rows, value_rows]).reshape(
        3, group_count, local_len, model_width
    )
    head_layout = lax.all_to_all(stacked, "seq", split_axis=3, concat_axis=2, tiled=True)
    seq_len = head_layout.shape[2]
    head_width = head_layout.shape[3]
    local_heads = head_width // HEAD_DIM
    block_rows = min(512, seq_len)
    block_count = seq_len // block_rows
    score_scale = HEAD_DIM ** (-0.5)

    def attend_forward(operands):
        seq_queries, seq_keys, seq_values, length = operands
        key_heads = seq_keys.reshape(seq_len, local_heads, HEAD_DIM)
        value_heads = seq_values.reshape(seq_len, local_heads, HEAD_DIM)
        key_live = jnp.arange(seq_len) < length

        def one_block(query_block):
            scores = (
                jnp.einsum(
                    "qhd,khd->hqk", query_block, key_heads, preferred_element_type=jnp.float32
                )
                * score_scale
            )
            scores = jnp.where(key_live[None, None, :], scores, masked_score)
            row_top = jnp.max(scores, axis=-1, keepdims=True)
            exponent = jnp.exp(scores - row_top)
            row_total = jnp.sum(exponent, axis=-1, keepdims=True)
            probabilities = (exponent / row_total).astype(jnp.bfloat16)
            context = jnp.einsum(
                "hqk,khd->qhd", probabilities, value_heads, preferred_element_type=jnp.float32
            )
            return (
                context.reshape(block_rows, head_width).astype(jnp.bfloat16),
                (row_top + jnp.log(row_total))[..., 0],
            )

        contexts, block_sums = lax.map(
            one_block, seq_queries.reshape(block_count, block_rows, local_heads, HEAD_DIM)
        )
        return (contexts.reshape(seq_len, head_width), block_sums)

    head_context, log_sums = lax.map(
        attend_forward, (head_layout[0], head_layout[1], head_layout[2], lengths)
    )
    context_rows = lax.all_to_all(
        head_context, "seq", split_axis=1, concat_axis=2, tiled=True
    ).reshape(row_count, model_width)
    attended = matmul_plain(context_rows, full_output) + bias_output
    first_sum = flat_in.astype(jnp.float32) + attended
    first_norm = layer_norm(first_sum, gain_first, shift_first).astype(jnp.bfloat16)
    up_pre = matmul_plain(first_norm, full_up) + bias_up
    hidden_act = gelu_exact(up_pre).astype(jnp.bfloat16)
    down_out = matmul_plain(hidden_act, full_down) + bias_down
    second_sum = first_norm.astype(jnp.float32) + down_out
    layer_out = layer_norm(second_sum, gain_second, shift_second).astype(jnp.bfloat16)
    regathered = (
        lax.all_gather(query_weight, "dp", axis=0, tiled=True),
        lax.all_gather(key_weight, "dp", axis=0, tiled=True),
        lax.all_gather(value_weight, "dp", axis=0, tiled=True),
        lax.all_gather(output_weight, "dp", axis=0, tiled=True),
        lax.all_gather(up_weight, "dp", axis=0, tiled=True),
        lax.all_gather(down_weight, "dp", axis=0, tiled=True),
        lax.all_gather(up_bias, "dp", axis=0, tiled=True),
    )
    full_query, full_key, full_value, full_output, full_up, full_down = regathered[0:6]
    bias_up = regathered[6].astype(jnp.float32)
    positions = lax.axis_index("seq") * local_len + jnp.arange(local_len)
    live_rows = (positions[None, :] < lengths[:, None]).reshape(row_count).astype(jnp.float32)
    grad_out = cotangent.reshape(row_count, model_width).astype(jnp.float32) * live_rows[:, None]
    norm_value, second_pull = jax.vjp(layer_norm, second_sum, gain_second, shift_second)
    second_sum_grad, second_gain_grad, second_shift_grad = second_pull(grad_out)
    down_grad_low = second_sum_grad.astype(jnp.bfloat16)
    down_weight_grad = inner_rows(hidden_act, down_grad_low)
    down_bias_grad = column_sums(down_grad_low)
    grad_hidden = times_transposed(down_grad_low, full_down)
    gelu_value, gelu_pull = jax.vjp(gelu_exact, up_pre)
    (up_grad_full,) = gelu_pull(grad_hidden)
    up_grad_low = up_grad_full.astype(jnp.bfloat16)
    up_weight_grad = inner_rows(first_norm, up_grad_low)
    up_bias_grad = column_sums(up_grad_low)
    first_norm_grad = second_sum_grad + times_transposed(up_grad_low, full_up)
    first_value, first_pull = jax.vjp(layer_norm, first_sum, gain_first, shift_first)
    first_sum_grad, first_gain_grad, first_shift_grad = first_pull(first_norm_grad)
    attended_low = first_sum_grad.astype(jnp.bfloat16)
    output_weight_grad = inner_rows(context_rows, attended_low)
    output_bias_grad = column_sums(attended_low)
    context_grad = times_transposed(attended_low, full_output).astype(jnp.bfloat16)
    grad_heads = lax.all_to_all(
        context_grad.reshape(group_count, local_len, model_width),
        "seq",
        split_axis=2,
        concat_axis=1,
        tiled=True,
    )

    def attend_backward(operands):
        seq_queries, seq_keys, seq_values, seq_grad, seq_sums, length = operands
        key_heads = seq_keys.reshape(seq_len, local_heads, HEAD_DIM)
        value_heads = seq_values.reshape(seq_len, local_heads, HEAD_DIM)
        key_live = jnp.arange(seq_len) < length

        def one_block(running, block_in):
            key_total, value_total = running
            query_block, grad_block, sum_block = block_in
            scores = (
                jnp.einsum(
                    "qhd,khd->hqk", query_block, key_heads, preferred_element_type=jnp.float32
                )
                * score_scale
            )
            scores = jnp.where(key_live[None, None, :], scores, masked_score)
            probabilities = jnp.exp(scores - sum_block[..., None])
            grad_probs = jnp.einsum(
                "qhd,khd->hqk", grad_block, value_heads, preferred_element_type=jnp.float32
            )
            row_delta = jnp.sum(probabilities * grad_probs, axis=-1, keepdims=True)
            grad_scores = (probabilities * (grad_probs - row_delta)).astype(jnp.bfloat16)
            query_grad = (
                jnp.einsum(
                    "hqk,khd->qhd", grad_scores, key_heads, preferred_element_type=jnp.float32
                )
                * score_scale
            )
            key_total = (
                key_total
                + jnp.einsum(
                    "hqk,qhd->khd", grad_scores, query_block, preferred_element_type=jnp.float32
                )
                * score_scale
            )
            value_total = value_total + jnp.einsum(
                "hqk,qhd->khd",
                probabilities.astype(jnp.bfloat16),
                grad_block,
                preferred_element_type=jnp.float32,
            )
            return (
                (key_total, value_total),
                query_grad.reshape(block_rows, head_width).astype(jnp.bfloat16),
            )

        zero_heads = jnp.zeros((seq_len, local_heads, HEAD_DIM), jnp.float32)
        block_shape = (block_count, block_rows, local_heads, HEAD_DIM)
        (key_total, value_total), query_grads = lax.scan(
            one_block,
            (zero_heads, zero_heads),
            (seq_queries.reshape(block_shape), seq_grad.reshape(block_shape), seq_sums),
        )
        return jnp.stack(
            [
                query_grads.reshape(seq_len, head_width),
                key_total.reshape(seq_len, head_width).astype(jnp.bfloat16),
                value_total.reshape(seq_len, head_width).astype(jnp.bfloat16),
            ]
        )

    head_grads = lax.map(
        attend_backward,
        (head_layout[0], head_layout[1], head_layout[2], grad_heads, log_sums, lengths),
    )
    row_grads = lax.all_to_all(head_grads, "seq", split_axis=2, concat_axis=3, tiled=True)
    query_grad_low = row_grads[:, 0].reshape(row_count, model_width)
    key_grad_low = row_grads[:, 1].reshape(row_count, model_width)
    value_grad_low = row_grads[:, 2].reshape(row_count, model_width)
    query_weight_grad = inner_rows(flat_in, query_grad_low)
    key_weight_grad = inner_rows(flat_in, key_grad_low)
    value_weight_grad = inner_rows(flat_in, value_grad_low)
    query_bias_grad = column_sums(query_grad_low)
    value_bias_grad = column_sums(value_grad_low)
    input_grad = (
        first_sum_grad
        + times_transposed(query_grad_low, full_query)
        + times_transposed(key_grad_low, full_key)
        + times_transposed(value_grad_low, full_value)
    ).astype(jnp.bfloat16)
    input_grad = input_grad.reshape(group_count, local_len, model_width)
    summed = (
        lax.psum_scatter(query_weight_grad, "dp", scatter_dimension=0, tiled=True),
        lax.psum_scatter(key_weight_grad, "dp", scatter_dimension=0, tiled=True),
        lax.psum_scatter(value_weight_grad, "dp", scatter_dimension=0, tiled=True),
        lax.psum_scatter(output_weight_grad, "dp", scatter_dimension=0, tiled=True),
        lax.psum_scatter(up_weight_grad, "dp", scatter_dimension=0, tiled=True),
        lax.psum_scatter(down_weight_grad, "dp", scatter_dimension=0, tiled=True),
        lax.psum_scatter(query_bias_grad, "dp", scatter_dimension=0, tiled=True),
        lax.psum_scatter(value_bias_grad, "dp", scatter_dimension=0, tiled=True),
        lax.psum_scatter(output_bias_grad, "dp", scatter_dimension=0, tiled=True),
        lax.psum_scatter(up_bias_grad, "dp", scatter_dimension=0, tiled=True),
        lax.psum_scatter(down_bias_grad, "dp", scatter_dimension=0, tiled=True),
        lax.psum_scatter(first_gain_grad, "dp", scatter_dimension=0, tiled=True),
        lax.psum_scatter(first_shift_grad, "dp", scatter_dimension=0, tiled=True),
        lax.psum_scatter(second_gain_grad, "dp", scatter_dimension=0, tiled=True),
        lax.psum_scatter(second_shift_grad, "dp", scatter_dimension=0, tiled=True),
    )
    totals = lax.psum(
        (
            summed[0],
            summed[1],
            summed[2],
            summed[3],
            summed[4],
            summed[5],
            summed[6],
            summed[7],
            summed[8],
            summed[9],
            summed[10],
            summed[11],
            summed[12],
            summed[13],
            summed[14],
        ),
        "seq",
    )
    layer_out = layer_out.reshape(group_count, local_len, model_width)
    return (
        layer_out,
        input_grad,
        totals[0],
        totals[1],
        totals[2],
        totals[3],
        totals[4],
        totals[5],
        totals[6],
        totals[7],
        totals[8],
        totals[9],
        totals[10],
        totals[11],
        totals[12],
        totals[13],
        totals[14],
    )


def solution(mesh):
    return jax.shard_map(
        local,
        mesh=mesh,
        in_specs=(
            P("dp", "seq", None),
            P("dp"),
            P("dp", None),
            P("dp", None),
            P("dp", None),
            P("dp", None),
            P("dp", None),
            P("dp", None),
            P("dp"),
            P("dp"),
            P("dp"),
            P("dp"),
            P("dp"),
            P("dp"),
            P("dp"),
            P("dp"),
            P("dp"),
            P("dp", "seq", None),
        ),
        out_specs=(
            P("dp", "seq", None),
            P("dp", "seq", None),
            P("dp", None),
            P("dp", None),
            P("dp", None),
            P("dp", None),
            P("dp", None),
            P("dp", None),
            P("dp"),
            P("dp"),
            P("dp"),
            P("dp"),
            P("dp"),
            P("dp"),
            P("dp"),
            P("dp"),
            P("dp"),
        ),
        check_vma=False,
    )
```

profile of v0, /device:TPU:0, one launch (start us, length us, event | category | flops | bytes accessed | tf_op | source)
XLA Modules:
  0.0 1238.4 jit_solution(14016261787662703552)
XLA Ops:
  19.3 39.9 %all-reduce.20 = (bf16[768]{0:T(1024)(128)(2,1)S(1)}, bf16[768]{0:T(1024)(128)(2,1)S(1)}, bf16[768]{0:T(1024)(128)(2,1)}, bf16[768]{0:T(1024)(128)(2,1)}, bf16[7...) all-reduce(bf16[768]{0:T(1024)(128)(2,1)S(1)} %dynamic-update-slice, ...), channel_id=1, replica_groups=mesh['dp'=8,'seq'=4] {'dp'}, use_global_device_ids=true, to_apply=%add.1 | all-reduce | flops 6144 | bytes 24576
  62.1 34.2 %all-gather.12.cloned.1.call-done = bf16[768,768]{1,0:T(8,128)(2,1)} async-done(((bf16[96,768]{1,0:T(8,128)(2,1)}), bf16[768,768]{1,0:T(8,128)(2,1)}) %all-gather.12.cloned.1.call-update) | async-done | bytes 1179664 | tf_op jit(solution)/shard_map/all_gather | solution.py:67
  99.0 39.3 %all-gather.10.cloned.1.call-done = bf16[768,768]{1,0:T(8,128)(2,1)} async-done(((bf16[96,768]{1,0:T(8,128)(2,1)}), bf16[768,768]{1,0:T(8,128)(2,1)}) %all-gather.10.cloned.1.call-update) | async-done | bytes 1179664 | tf_op jit(solution)/shard_map/all_gather | solution.py:66
  149.7 27.9 %all-to-all-done = bf16[3,2,256,768]{2,1,0,3:T(2,128)(2,1)S(1)} async-done(((bf16[3,2,256,768]{2,1,0,3:T(2,128)(2,1)}), bf16[3,2,256,768]{2,1,0,3:T(2,128)(2,1)S(1)}, u32[]{:S(2)}, u32[]{:S(2)}) %all-to-all-start) | async-done | bytes 2359328 | tf_op jit(solution)/shard_map/all_to_all | solution.py:100
  183.4 29.9 %while.51 = (s32[]{:T(128)}, bf16[2,1024,192]{2,1,0:T(8,128)(2,1)}, f32[2,2,3,512]{3,2,1,0:T(4,128)S(1)}, bf16[2,1024,192]{1,2,0:T(8,128)(2,1)}, bf16[2,1024,192...) while((s32[]{:T(128)}, bf16[2,1024,192]{2,1,0:T(8,128)(2,1)}, ...), condition=%wide.region_5.6_spmd, body=%wide.region_0.5_spmd.sunk | while | flops 421625344 | bytes 26176296 | solution.py:139
  186.4 10.9 while.54
  201.4 10.9 while.54
  220.4 26.8 %all-gather = bf16[8,1,384]{2,1,0:T(2,128)(2,1)S(1)} all-gather(bf16[1,1,384]{2,1,0:T(2,128)(2,1)S(1)} %reshape.301), channel_id=1, replica_groups=mesh['dp'=8,'seq'=4] {'dp'}, dimensions={0}, use_global_device_ids=true | all-gather | bytes 6912 | tf_op jit(solution)/shard_map/all_gather | solution.py:74
  261.3 20.9 %multiply_convert_fusion.1 = (bf16[512,3072]{1,0:T(8,128)(2,1)}, f32[512,3072]{1,0:T(8,128)}, f32[512,3072]{1,0:T(8,128)}) fusion(f32[3072]{0:T(1024)S(1)} %bitcast.268, bf16[768,3072]{1,0:T(8,128)(2,1)} %all-gather.16.cloned.1.call-done, f32[512,768]{1,0:T(8,128)} %copy-done.21, f32[768]{0:T(1024)S(1)} %convert_element_type.180, ...), kind=kOutput, calls=%fused_computation.66 | convolution fusion | flops 2521694208 | bytes 22042624 | tf_op jit(solution)/shard_map/dot_general | solution.py:25
  282.2 59.2 %all-gather.18.cloned.1.call-done = bf16[3072,768]{1,0:T(8,128)(2,1)} async-done(((bf16[384,768]{1,0:T(8,128)(2,1)}), bf16[3072,768]{1,0:T(8,128)(2,1)}) %all-gather.18.cloned.1.call-update) | async-done | bytes 4718608 | tf_op jit(solution)/shard_map/all_gather | solution.py:70
  374.1 11.6 all-to-all-done.2
  385.9 70.7 %while.53 = (s32[]{:T(128)}, bf16[2,3,1024,192]{2,3,1,0:T(8,128)(2,1)}, bf16[2,1024,192]{1,2,0:T(8,128)(2,1)}, bf16[2,1024,192]{1,2,0:T(8,128)(2,1)S(1)}, f32[2,...) while((s32[]{:T(128)}, ...), condition=%wide.region_18.19_spmd, body=%wide.region_14.18_spmd.sunk | while | flops 1035337216 | bytes 144484816 | solution.py:254
  389.2 27.8 %while.55 = (s32[]{:T(128)}, f32[1024,3,64]{0,2,1:T(8,128)}, f32[1024,3,64]{0,2,1:T(8,128)}, bf16[2,512,192]{1,2,0:T(8,128)(2,1)}, bf16[2,512,3,64]{1,3,2,0:T(8,...) while((s32[]{:T(128)}, f32[1024,3,64]{0,2,1:T(8,128)}, ...), condition=%wide.region_17.17_spmd.clone, body=%wide.region_15.16_spmd.clone.sunk | while | flops 1031405056 | bytes 115951104 | solution.py:241
  424.4 27.8 %while.55 = (s32[]{:T(128)}, f32[1024,3,64]{0,2,1:T(8,128)}, f32[1024,3,64]{0,2,1:T(8,128)}, bf16[2,512,192]{1,2,0:T(8,128)(2,1)}, bf16[2,512,3,64]{1,3,2,0:T(8,...) while((s32[]{:T(128)}, f32[1024,3,64]{0,2,1:T(8,128)}, ...), condition=%wide.region_17.17_spmd.clone, body=%wide.region_15.16_spmd.clone.sunk | while | flops 1031405056 | bytes 115951104 | solution.py:241
  464.1 40.3 %all_to_all.66 = bf16[2,3,1024,192]{3,0,1,2:T(2,128)(2,1)} all-to-all(bf16[2,3,1024,192]{3,0,1,2:T(2,128)(2,1)S(1)} %copy.120), channel_id=1, replica_groups=mesh['dp'=8,'seq'=4] {'seq'}, dimensions={2} | all-to-all | bytes 4718592 | tf_op jit(solution)/shard_map/all_to_all | solution.py:258
  504.3 9.0 copy.129
  564.0 28.1 %reduce-scatter.19.cloned.1.call-done = f32[96,768]{1,0:T(8,128)} async-done(((f32[768,768]{1,0:T(8,128)}), f32[96,768]{1,0:T(8,128)}) %reduce-scatter.19.cloned.1.call-update) | async-done | bytes 294928
  594.0 69.7 %reduce-scatter.21.cloned.1.call-done = f32[96,768]{1,0:T(8,128)} async-done(((f32[768,768]{1,0:T(8,128)}), f32[96,768]{1,0:T(8,128)}) %reduce-scatter.21.cloned.1.call-update) | async-done | bytes 294928
  665.6 69.7 %reduce-scatter.23.cloned.1.call-done = f32[96,768]{1,0:T(8,128)} async-done(((f32[768,768]{1,0:T(8,128)}), f32[96,768]{1,0:T(8,128)}) %reduce-scatter.23.cloned.1.call-update) | async-done | bytes 294928
  737.2 69.5 %reduce-scatter.13.cloned.1.call-done = f32[96,768]{1,0:T(8,128)} async-done(((f32[768,768]{1,0:T(8,128)}), f32[96,768]{1,0:T(8,128)}) %reduce-scatter.13.cloned.1.call-update) | async-done | bytes 294928 | tf_op jit(solution)/shard_map/reduce_scatter | solution.py:278
  806.8 166.1 %reduce-scatter.15.cloned.1.call-done = f32[96,3072]{1,0:T(8,128)} async-done(((f32[768,3072]{1,0:T(8,128)}), f32[96,3072]{1,0:T(8,128)}) %reduce-scatter.15.cloned.1.call-update) | async-done | bytes 1179664 | tf_op jit(solution)/shard_map/reduce_scatter | solution.py:279
  972.9 166.0 %reduce-scatter.17.cloned.1.call-done = f32[384,768]{1,0:T(8,128)} async-done(((f32[3072,768]{1,0:T(8,128)}), f32[384,768]{1,0:T(8,128)}) %reduce-scatter.17.cloned.1.call-update) | async-done | bytes 1179664 | tf_op jit(solution)/shard_map/reduce_scatter | solution.py:280
  1142.0 35.7 %all-reduce.17 = (f32[768]{0:T(1024)S(1)}, f32[768]{0:T(1024)S(1)}, f32[768]{0:T(1024)S(1)}, f32[3072]{0:T(1024)S(1)}, f32[768]{0:T(1024)S(1)}, /*index=5*/f32[7...) all-reduce(f32[768]{0:T(1024)S(1)} %get-tuple-element.403, ...), channel_id=8, replica_groups=mesh['dp'=8,'seq'=4] {'dp'}, use_global_device_ids=true, to_apply=%region_32.33.clone | all-reduce | flops 9216 | bytes 73728
  1191.2 31.0 %all-reduce.23.cloned.1.call-done = (f32[96,768]{0,1:T(8,128)}, f32[96,768]{0,1:T(8,128)}, f32[96,768]{0,1:T(8,128)}, f32[96,768]{1,0:T(8,128)}, f32[96,3072]{1,0:T(8,128)}, /*index=5*/f32[384,768]{1,0:T(8,128)}) async-done(((f32[96,768]{0,1:T(8,128)}, f32[96,768]{0,1:T(8,128)}, f32[96,768]{0,1:T(8,128)}, f32[96,768]{1,0:T(8,128)}, f32[96,3072]{1,0:T(8,128)}, /*index=5*/f32[384,768]{1,0:T(8,128)}), ...) | async-done | bytes 3538960 | tf_op jit(solution)/shard_map/psum | solution.py:291
  (473 shorter events, 275.2 us)
Async XLA Ops:
  7.2 52.0 %all-gather.8.cloned.1.call-start = ((), (), s32[]{:S(2)}) async-start(), calls=%async_computation.10 | async-start | bytes 1327104 | tf_op jit(solution)/shard_map/all_gather | solution.py:65
  7.9 88.4 %all-gather.12.cloned.1.call-start = ((), (), s32[]{:S(2)}) async-start(), calls=%async_computation.12 | async-start | bytes 1327104 | tf_op jit(solution)/shard_map/all_gather | solution.py:67
  8.7 129.7 %all-gather.10.cloned.1.call-start = ((), (), s32[]{:S(2)}) async-start(), calls=%async_computation.11 | async-start | bytes 1327104 | tf_op jit(solution)/shard_map/all_gather | solution.py:66
  9.4 240.4 %all-gather.14.cloned.1.call-start = ((), (), s32[]{:S(2)}) async-start(), calls=%async_computation.13 | async-start | bytes 1327104 | tf_op jit(solution)/shard_map/all_gather | solution.py:68
  10.0 251.3 %all-gather.16.cloned.1.call-start = ((), (), s32[]{:S(2)}) async-start(), calls=%async_computation.14 | async-start | bytes 5308416 | tf_op jit(solution)/shard_map/all_gather | solution.py:69
  145.4 32.1 %all-to-all-start = ((bf16[3,2,256,768]{2,1,0,3:T(2,128)(2,1)}), bf16[3,2,256,768]{2,1,0,3:T(2,128)(2,1)S(1)}, u32[]{:S(2)}, u32[]{:S(2)}) async-start(bf16[3,2,256,768]{2,1,0,3:T(2,128)(2,1)} %pad_maximum_fusion), calls=%async_computation | async-start | bytes 4718592 | tf_op jit(solution)/shard_map/all_to_all | solution.py:100
  149.1 192.3 %all-gather.18.cloned.1.call-start = ((), (), s32[]{:S(2)}) async-start(), calls=%async_computation.15 | async-start | bytes 5308416 | tf_op jit(solution)/shard_map/all_gather | solution.py:70
  216.7 31.3 %all-to-all-start.1 = ((bf16[2,1024,192]{2,0,1:T(2,128)(2,1)}), bf16[2,1024,192]{2,0,1:T(2,128)(2,1)S(1)}, u32[]{:S(2)}, u32[]{:S(2)}) async-start(bf16[2,1024,192]{2,0,1:T(2,128)(2,1)} %copy.115), calls=%async_computation.1 | async-start | bytes 2097152 | tf_op jit(solution)/shard_map/all_to_all | solution.py:142
  220.4 144.1 %copy-start.41 = (f32[768]{0:T(1024)}, f32[768]{0:T(1024)S(1)}, u32[]{:S(2)}) copy-start(f32[768]{0:T(1024)S(1)} %convert_element_type.179) | copy-start | bytes 9220
  370.5 15.1 %all-to-all-start.2 = ((bf16[2,256,768]{1,0,2:T(2,128)(2,1)}), bf16[2,256,768]{1,0,2:T(2,128)(2,1)S(1)}, u32[]{:S(2)}, u32[]{:S(2)}) async-start(bf16[2,256,768]{1,0,2:T(2,128)(2,1)} %copy.117), calls=%async_computation.2 | async-start | bytes 1572864 | tf_op jit(solution)/shard_map/all_to_all | solution.py:185
  374.0 218.1 %reduce-scatter.19.cloned.1.call-start = ((), (), s32[]{:S(2)}) async-start(), calls=%async_computation.19 | async-start | bytes 2654208
  525.7 138.0 %reduce-scatter.21.cloned.1.call-start = ((), (), s32[]{:S(2)}) async-start(), calls=%async_computation.20 | async-start | bytes 2654208
  534.4 200.9 %reduce-scatter.23.cloned.1.call-start = ((), (), s32[]{:S(2)}) async-start(), calls=%async_computation.21 | async-start | bytes 2654208
  542.7 264.1 %reduce-scatter.13.cloned.1.call-start = ((), (), s32[]{:S(2)}) async-start(), calls=%async_computation.16 | async-start | bytes 2654208 | tf_op jit(solution)/shard_map/reduce_scatter | solution.py:278
  546.4 426.5 %reduce-scatter.15.cloned.1.call-start = ((), (), s32[]{:S(2)}) async-start(), calls=%async_computation.17 | async-start | bytes 10616832 | tf_op jit(solution)/shard_map/reduce_scatter | solution.py:279
  555.4 583.5 %reduce-scatter.17.cloned.1.call-start = ((), (), s32[]{:S(2)}) async-start(), calls=%async_computation.18 | async-start | bytes 10616832 | tf_op jit(solution)/shard_map/reduce_scatter | solution.py:280
  563.9 576.3 %copy-start.46 = (f32[2,256]{1,0:T(2,128)S(1)}, f32[2,256]{1,0:T(2,128)}, u32[]{:S(2)}) copy-start(f32[2,256]{1,0:T(2,128)} %get-tuple-element.530) | copy-start | bytes 6148
  564.0 658.2 %all-reduce.23.cloned.1.call-start = ((), (), s32[]{:S(2)}) async-start(), calls=%async_computation.22 | async-start | bytes 7667712 | tf_op jit(solution)/shard_map/psum | solution.py:291
  737.2 404.7 %copy-start.38 = (f32[768]{0:T(1024)S(1)}, f32[768]{0:T(1024)}, u32[]{:S(2)}) copy-start(f32[768]{0:T(1024)} %get-tuple-element.400) | copy-start | bytes 9220
  737.2 404.7 %copy-start.39 = (f32[768]{0:T(1024)S(1)}, f32[768]{0:T(1024)}, u32[]{:S(2)}) copy-start(f32[768]{0:T(1024)} %get-tuple-element.501) | copy-start | bytes 9220
  737.2 404.7 %copy-start.40 = (f32[768]{0:T(1024)S(1)}, f32[768]{0:T(1024)}, u32[]{:S(2)}) copy-start(f32[768]{0:T(1024)} %get-tuple-element.505) | copy-start | bytes 9220
  737.2 404.7 %copy-start.43 = (f32[3072]{0:T(1024)S(1)}, f32[3072]{0:T(1024)}, u32[]{:S(2)}) copy-start(f32[3072]{0:T(1024)} %get-tuple-element.503) | copy-start | bytes 36868
  737.2 404.7 %copy-start.49 = (f32[768]{0:T(1024)S(1)}, f32[768]{0:T(1024)}, u32[]{:S(2)}) copy-start(f32[768]{0:T(1024)} %get-tuple-element.398) | copy-start | bytes 9220
  737.2 404.7 %copy-start.50 = (f32[768]{0:T(1024)S(1)}, f32[768]{0:T(1024)}, u32[]{:S(2)}) copy-start(f32[768]{0:T(1024)} %get-tuple-element.404) | copy-start | bytes 9220
  (99 other events, 991.2 us)
Sparse Core Ops, SparseCore 0:
  10.2 43.9 all-gather.7
  56.4 39.8 all-gather.11
  98.5 39.8 all-gather.9
  140.4 39.8 all-gather.13
  182.4 78.8 all-gather.15
  263.3 78.0 all-gather.17
  525.8 66.2 reduce-scatter.18
  595.6 68.0 reduce-scatter.20
  667.2 68.0 reduce-scatter.22
  738.7 68.0 reduce-scatter.12
  810.4 162.4 reduce-scatter.14
  976.3 162.5 reduce-scatter.16
  1142.3 79.8 all-reduce.22
where the time goes:
time: 1250 us; the launch traced here: 1240 us
  waiting for transfers between devices  784 us (63%)
  blocking collectives  149 us (12%)
  matrix products  141 us (11%)
  local copies, waits for them, and re-layouts  98.8 us (8%)
  other arithmetic  36 us (3%)
  between operations  16.9 us (1%)
    unnamed x16, waiting for transfers between devices  171 us
    reduce_scatter x1, waiting for transfers between devices, local(): lax.psum_scatter(up_weight_grad, 'dp', scatter_dimension=0, tiled=True)  166 us
    reduce_scatter x1, waiting for transfers between devices, local(): lax.psum_scatter(down_weight_grad, 'dp', scatter_dimension=0, tiled=True)  166 us
    unnamed x2, blocking collectives  75.6 us
    reduce_scatter x1, waiting for transfers between devices, local(): lax.psum_scatter(output_weight_grad, 'dp', scatter_dimension=0, tiled=True)  69.5 us
    all_gather x1, waiting for transfers between devices, local(): lax.all_gather(down_weight, 'dp', axis=0, tiled=True)  59.2 us
    all_to_all x1, blocking collectives, local(): lax.all_to_all(head_grads, 'seq', split_axis=2, concat_axis=3, tiled=True)  40.3 us
    all_gather x1, waiting for transfers between devices, local(): lax.all_gather(key_weight, 'dp', axis=0, tiled=True)  39.3 us
  transfers between devices with their start and end apart: 16, of which 13 were waited for; matrix products, arithmetic and copies ran while one was open for 11% of the time, Pallas kernels for 0%

commit v1 on v0

v1 whole, which is shorter than its diff:
```python
import functools
import jax
import jax.numpy as jnp
from jax import lax
from jax.experimental import pallas as pl
from jax.experimental.pallas import tpu as pltpu
from jax.sharding import PartitionSpec as P

MESH = pl.DeviceIdType.MESH
HEAD_DIM = 64
eps_norm = 1e-05
masked_score = -1000000000.0


def flip(value, bits):
    bit = 1
    while bit <= bits:
        if bits & bit:
            value = value + bit - 2 * bit * lax.rem(lax.div(value, bit), 2)
        bit *= 2
    return value


class Place:
    def __init__(self, dp_size):
        self.dp = lax.axis_index("dp")
        self.seq = lax.axis_index("seq")
        self.depth = dp_size // 2
        self.z = lax.div(self.dp, 2)
        self.y = lax.rem(self.dp, 2)
        self.core = lax.rem(self.seq, 2)
        self.side = lax.div(self.seq, 2)

    def along_z(self, k):
        return flip(self.dp, 2 * k)

    def peers(self):
        result = [(self.along_z(k), self.seq) for k in range(1, self.depth)]
        result.append((flip(self.dp, 1), self.seq))
        result.append((self.dp, flip(self.seq, 1)))
        result.append((self.dp, flip(self.seq, 2)))
        return result

    def greet(self):
        barrier = pltpu.get_barrier_semaphore()
        peers = self.peers()
        for peer in peers:
            pl.semaphore_signal(barrier, inc=1, device_id=peer, device_id_type=MESH)
        pl.semaphore_wait(barrier, len(peers))


class Gather:
    def __init__(self, place, src, dst, rows, columns, to_columns, sems):
        self.place, self.src, self.dst = place, src, dst
        self.columns, self.to_columns = columns, to_columns
        self.first, count = rows
        self.send, self.recv, self.local = sems
        self.depth = place.depth
        unit = count // 6
        self.fetch = (place.core * (3 * unit) + place.side * unit, 2 * unit)
        self.far = (place.core * (3 * unit) + place.side * (2 * unit), unit)
        self.got = (place.core * (3 * unit) + (1 - place.side) * (2 * unit), unit)
        self.half = (place.core * (3 * unit), 3 * unit)

    def view(self, z, y, window):
        rows = pl.ds(pl.multiple_of(self.first + window[0], window[1] if window[1] < 32 else 16), window[1])
        return self.dst.at[z, y, rows, pl.ds(*self.to_columns)]

    def copy(self, src, dst, index, peer):
        return pltpu.make_async_remote_copy(
            src_ref=src, dst_ref=dst, send_sem=self.send.at[index], recv_sem=self.recv.at[index],
            device_id=peer, device_id_type=MESH,
        )

    def mine(self):
        rows = pl.ds(pl.multiple_of(self.first + self.fetch[0], 16), self.fetch[1])
        return self.src.at[rows, pl.ds(*self.columns)]

    def own(self):
        p = self.place
        return pltpu.make_async_copy(self.mine(), self.view(p.z, p.y, self.fetch), self.local)

    def over_z(self, k):
        p = self.place
        return self.copy(self.mine(), self.view(p.z, p.y, self.fetch), k, (p.along_z(k), p.seq))

    def over_y(self):
        p = self.place
        ref = self.view(slice(None), p.y, self.fetch)
        return self.copy(ref, ref, 0, (flip(p.dp, 1), p.seq))

    def over_x(self):
        p, every = self.place, slice(None)
        ref = self.view(every, every, self.far)
        return self.copy(ref, ref, self.depth, (p.dp, flip(p.seq, 2)))

    def across(self):
        p, every = self.place, slice(None)
        ref = self.view(every, every, self.half)
        return self.copy(ref, ref, self.depth + 1, (p.dp, flip(p.seq, 1)))

    def stage_z(self):
        self.own().start()
        for k in range(1, self.depth):
            self.over_z(k).start()

    def stage_y(self):
        self.own().wait()
        for k in range(1, self.depth):
            self.over_z(k).wait_recv()
        self.over_y().start()

    def stage_x(self):
        self.over_y().wait_recv()
        self.over_x().start()

    def stage_core(self):
        self.over_x().wait_recv()
        self.across().start()

    def finish(self):
        for k in range(1, self.depth):
            self.over_z(k).wait_send()
        self.over_y().wait_send()
        self.over_x().wait_send()
        self.across().wait()


def gather_sems(dp_size, units):
    n = dp_size // 2 + 2
    return [pltpu.SemaphoreType.DMA((units, n)), pltpu.SemaphoreType.DMA((units, n)), pltpu.SemaphoreType.DMA((units,))]


class Spread:
    def __init__(self, place, src, dst, sems):
        self.place, self.src, self.dst = place, src, dst
        self.send, self.recv, self.local = sems

    def own(self):
        return pltpu.make_async_copy(self.src, self.dst.at[self.place.z, self.place.y], self.local)

    def over_z(self, k):
        p = self.place
        return pltpu.make_async_remote_copy(
            src_ref=self.src, dst_ref=self.dst.at[p.z, p.y], send_sem=self.send.at[k], recv_sem=self.recv.at[k],
            device_id=(p.along_z(k), p.seq), device_id_type=MESH,
        )

    def over_y(self):
        p = self.place
        ref = self.dst.at[:, p.y]
        return pltpu.make_async_remote_copy(
            src_ref=ref, dst_ref=ref, send_sem=self.send.at[0], recv_sem=self.recv.at[0],
            device_id=(flip(p.dp, 1), p.seq), device_id_type=MESH,
        )

    def start(self):
        self.own().start()
        for k in range(1, self.place.depth):
            self.over_z(k).start()

    def forward(self):
        self.own().wait()
        for k in range(1, self.place.depth):
            self.over_z(k).wait_recv()
        self.over_y().start()

    def finish(self):
        for k in range(1, self.place.depth):
            self.over_z(k).wait_send()
        self.over_y().wait()


def gather_steps(units, window):
    count = len(units)
    steps = [[unit.stage_z for unit in units[:window]]]
    for i in range(count + 4):
        step = []
        if 0 <= i - 4 < count:
            step.append(units[i - 4].stage_core)
        if 0 <= i - 2 < count:
            step.append(units[i - 2].stage_x)
        if i < count:
            step.append(units[i].stage_y)
            if i + window < count:
                step.append(units[i + window].stage_z)
        steps.append(step)
    steps.append([unit.finish for unit in units])
    return steps


class Swap:
    def __init__(self, place, src, dst, send, recv, local):
        side = place.side
        length = src.shape[1]
        own = dst.at[pl.ds(pl.multiple_of(side * length, 8), length)]
        self.here = pltpu.make_async_copy(src.at[side], own, local)
        self.there = pltpu.make_async_remote_copy(
            src_ref=src.at[1 - side], dst_ref=own, send_sem=send, recv_sem=recv,
            device_id=(place.dp, flip(place.seq, 2)), device_id_type=MESH,
        )

    def start(self):
        self.here.start()
        self.there.start()

    def wait(self):
        self.here.wait()
        self.there.wait()


def weight_units(place, srcs, dsts, plan, sems):
    send, recv, local = sems
    return [
        Gather(place, srcs[s], dsts[d], (first, rows), (column, width), (to, width), (send.at[i], recv.at[i], local.at[i]))
        for i, (s, d, first, rows, column, width, to) in enumerate(plan)
    ]


def first_kernel(dp_size, plan, n_src, n_dst, n_rows, window, *refs):
    refs = list(refs)
    srcs, vec, rows_in = refs[:n_src], refs[n_src], refs[n_src + 1:n_src + 1 + n_rows]
    refs = refs[n_src + 1 + n_rows:]
    dsts, vec_out, rows_out = refs[:n_dst], refs[n_dst], refs[n_dst + 1:n_dst + 1 + n_rows]
    send, recv, local, vec_send, vec_recv, swap_sem, vec_local = refs[n_dst + 1 + n_rows:]
    place = Place(dp_size)
    place.greet()
    moves = [Swap(place, a, b, swap_sem.at[i, 0], swap_sem.at[i, 1], swap_sem.at[i, 2]) for i, (a, b) in enumerate(zip(rows_in, rows_out))]
    spread = Spread(place, vec, vec_out, (vec_send, vec_recv, vec_local))
    units = weight_units(place, srcs, dsts, plan, (send, recv, local))
    spread.start()
    for move in moves:
        move.start()
    steps = gather_steps(units, window)
    for call in steps[0]:
        call()
    spread.forward()
    for step in steps[1:]:
        for call in step:
            call()
    spread.finish()
    for move in moves:
        move.wait()


def first_exchange(dp_size, weights, dst_shapes, plan, vec, rows, window=3):
    n_src, n_dst = len(weights), len(dst_shapes)
    anywhere = pl.BlockSpec(memory_space=pl.ANY)
    z = dp_size // 2
    out_shape = [jax.ShapeDtypeStruct((z, 2, *shape), jnp.bfloat16) for shape in dst_shapes]
    out_shape += [jax.ShapeDtypeStruct((z, 2, *vec.shape), vec.dtype)]
    out_shape += [jax.ShapeDtypeStruct((r.shape[0] * r.shape[1], r.shape[2]), r.dtype) for r in rows]
    return pl.pallas_call(
        functools.partial(first_kernel, dp_size, plan, n_src, n_dst, len(rows), window),
        out_shape=out_shape,
        in_specs=[anywhere] * (n_src + 1 + len(rows)),
        out_specs=[anywhere] * (n_dst + 1 + len(rows)),
        scratch_shapes=gather_sems(dp_size, len(plan)) + [pltpu.SemaphoreType.DMA((z,))] * 2 + [pltpu.SemaphoreType.DMA((len(rows), 3)), pltpu.SemaphoreType.DMA],
        compiler_params=pltpu.CompilerParams(collective_id=0, has_side_effects=True),
        name="first_exchange",
    )(*weights, vec, *rows)


class Reduce:
    def __init__(self, place, src, rows, columns, to_columns, out, to_row, bufs, sems):
        self.place, self.src, self.out = place, src, out
        self.columns, self.to_columns, self.to_row = columns, to_columns, to_row
        self.first, count = rows
        self.unit = unit = count // 6
        self.own, self.from_core, self.to_x, self.from_x, self.to_y, self.from_y, self.to_z, self.from_z, self.last, self.got, self.total = bufs
        self.send, self.recv = sems
        self.depth = place.depth
        self.half = place.core * (3 * unit)
        self.sibling_half = (1 - place.core) * (3 * unit)

    def view(self, start):
        rows = pl.ds(pl.multiple_of(self.first + start, self.unit), 3 * self.unit)
        return self.src.at[:, :, rows, pl.ds(*self.columns)]

    def copy(self, src, dst, index, peer):
        return pltpu.make_async_remote_copy(
            src_ref=src, dst_ref=dst, send_sem=self.send.at[index], recv_sem=self.recv.at[index],
            device_id=peer, device_id_type=MESH,
        )

    def load(self):
        return pltpu.make_async_copy(self.view(self.half), self.own, self.send.at[0])

    def core(self):
        p = self.place
        return self.copy(self.view(self.sibling_half), self.from_core, self.depth, (p.dp, flip(p.seq, 1)))

    def x(self):
        p = self.place
        return self.copy(self.to_x, self.from_x, self.depth + 1, (p.dp, flip(p.seq, 2)))

    def y(self):
        p = self.place
        return self.copy(self.to_y, self.from_y, self.depth + 2, (flip(p.dp, 1), p.seq))

    def z(self, k):
        p = self.place
        return self.copy(self.to_z.at[k - 1], self.from_z.at[k - 1], k, (p.along_z(k), p.seq))

    def x_last(self):
        p = self.place
        return self.copy(self.last, self.got, self.depth + 3, (p.dp, flip(p.seq, 2)))

    def place_out(self):
        row = pl.multiple_of(self.to_row + self.half, self.unit)
        return self.out.at[pl.ds(row, 3 * self.unit), pl.ds(*self.to_columns)]

    def put_here(self):
        return pltpu.make_async_copy(self.total, self.place_out(), self.send.at[self.depth + 5])

    def put_there(self):
        p = self.place
        return self.copy(self.total, self.place_out(), self.depth + 4, (p.dp, flip(p.seq, 1)))

    def rows(self, start):
        return pl.ds(pl.multiple_of(start, self.unit), self.unit)

    def stage_core(self):
        self.load().start()
        self.core().start()

    def chip(self, z, y, start):
        rows = self.rows(start)
        return self.own[z, y, rows, :].astype(jnp.float32) + self.from_core[z, y, rows, :].astype(jnp.float32)

    def stage_x(self):
        self.load().wait()
        self.core().wait_recv()
        u, side, y = self.unit, self.place.side, self.place.y
        far = (1 - side) * (2 * u)

        def body(z, carry):
            for yy in range(2):
                self.to_x[z, yy, :, :] = self.chip(z, yy, far).astype(jnp.bfloat16)
            return carry

        lax.fori_loop(0, self.depth, body, 0)
        self.x().start()

    def pair(self, z, y):
        u = self.unit
        solo = self.chip(z, y, self.place.side * (2 * u)) + self.from_x[z, y, :, :].astype(jnp.float32)
        return self.chip(z, y, u), solo

    def stage_y(self):
        self.x().wait_recv()
        u, y = self.unit, self.place.y

        def body(z, carry):
            both, solo = self.pair(z, 1 - y)
            self.to_y[z, pl.ds(0, u), :] = both.astype(jnp.bfloat16)
            self.to_y[z, pl.ds(u, u), :] = solo.astype(jnp.bfloat16)
            return carry

        lax.fori_loop(0, self.depth, body, 0)
        self.y().start()

    def column(self, z):
        u = self.unit
        both, solo = self.pair(z, self.place.y)
        both = both + self.from_y[z, pl.ds(0, u), :].astype(jnp.float32)
        solo = solo + self.from_y[z, pl.ds(u, u), :].astype(jnp.float32)
        return both, solo

    def stage_z(self):
        self.y().wait_recv()
        u = self.unit
        for k in range(1, self.depth):
            both, solo = self.column(flip(self.place.z, k))
            self.to_z[k - 1, pl.ds(0, u), :] = both.astype(jnp.bfloat16)
            self.to_z[k - 1, pl.ds(u, u), :] = solo.astype(jnp.bfloat16)
            self.z(k).start()

    def stage_last(self):
        for k in range(1, self.depth):
            self.z(k).wait_recv()
        u = self.unit
        both, solo = self.column(self.place.z)
        for k in range(1, self.depth):
            both = both + self.from_z[k - 1, pl.ds(0, u), :].astype(jnp.float32)
            solo = solo + self.from_z[k - 1, pl.ds(u, u), :].astype(jnp.float32)
        self.last[pl.ds(0, u), :] = both.astype(jnp.bfloat16)
        self.last[pl.ds(u, u), :] = solo.astype(jnp.bfloat16)
        self.x_last().start()

    def stage_out(self):
        self.x_last().wait_recv()
        u, side = self.unit, self.place.side
        mine, got = self.last[...].astype(jnp.float32), self.got[...].astype(jnp.float32)
        self.total[self.rows(u), :] = mine[:u] + got[:u]
        self.total[self.rows(side * (2 * u)), :] = mine[u:]
        self.total[self.rows((1 - side) * (2 * u)), :] = got[u:]
        self.put_here().start()
        self.put_there().start()

    def finish(self):
        self.core().wait_send()
        self.x().wait_send()
        self.y().wait_send()
        for k in range(1, self.depth):
            self.z(k).wait_send()
        self.x_last().wait_send()
        self.put_here().wait()
        self.put_there().wait()


def reduce_scratch(dp_size, units, rows, width):
    z, u = dp_size // 2, rows // 6
    low = lambda *shape: pltpu.VMEM((units, *shape, width), jnp.bfloat16)
    return [
        low(z, 2, 3 * u), low(z, 2, 3 * u), low(z, 2, u), low(z, 2, u), low(z, 2 * u), low(z, 2 * u),
        low(z - 1, 2 * u), low(z - 1, 2 * u), low(2 * u), low(2 * u), pltpu.VMEM((units, 3 * u, width), jnp.float32),
        pltpu.SemaphoreType.DMA((units, z + 6)), pltpu.SemaphoreType.DMA((units, z + 6)),
    ]


def reduce_units(place, srcs, outs, plan, scratch):
    bufs, send, recv = scratch[:-2], scratch[-2], scratch[-1]
    return [
        Reduce(place, srcs[s], (first, rows), (column, width), (to, width), outs[o], to_row, [b.at[i] for b in bufs], (send.at[i], recv.at[i]))
        for i, (s, o, first, rows, column, width, to_row, to) in enumerate(plan)
    ]


STAGES = ("stage_core", "stage_x", "stage_y", "stage_z", "stage_last", "stage_out", "finish")


def reduce_steps(units, ages=(0, 1, 3, 5, 7, 9, 11)):
    steps = []
    for tick in range(len(units) + ages[-1]):
        step = []
        for stage, age in sorted(zip(STAGES, ages), key=lambda pair: -pair[1]):
            i = tick - age
            if 0 <= i < len(units):
                step.append(getattr(units[i], stage))
        steps.append(step)
    return steps


class SumAll:
    def __init__(self, place, src, out, buf, got, send, recv):
        self.place, self.src, self.out, self.buf, self.got, self.send, self.recv = place, src, out, buf, got, send, recv

    def copy(self, stage, slot, peer):
        return pltpu.make_async_remote_copy(
            src_ref=self.buf.at[stage], dst_ref=self.got.at[slot], send_sem=self.send.at[slot], recv_sem=self.recv.at[slot],
            device_id=peer, device_id_type=MESH,
        )

    def copies(self, stage):
        p = self.place
        if stage < 3:
            peer = [(p.dp, flip(p.seq, 1)), (p.dp, flip(p.seq, 2)), (flip(p.dp, 1), p.seq)][stage]
            return [self.copy(stage, stage, peer)]
        return [self.copy(3, 2 + k, (p.along_z(k), p.seq)) for k in range(1, p.depth)]

    def begin(self):
        self.buf[0] = self.src[...]
        for c in self.copies(0):
            c.start()

    def advance(self, stage):
        for c in self.copies(stage):
            c.wait_recv()
        if stage < 3:
            self.buf[stage + 1] = self.buf[stage] + self.got[stage]
            for c in self.copies(stage + 1):
                c.start()
        else:
            z, n = self.place.z, self.place.depth
            pick = lambda i: i
            total = self.buf[3]
            parts = [self.buf[3]] + [self.got[2 + k] for k in range(1, n)]
            total = (parts[0] + parts[1]) + (parts[2] + parts[3])
            self.out[...] = total

    def finish(self):
        for stage in range(4):
            for c in self.copies(stage):
                c.wait_send()


def last_kernel(dp_size, plan, n_src, n_out, n_rows, *refs):
    refs = list(refs)
    srcs, vec, rows_in = refs[:n_src], refs[n_src], refs[n_src + 1:n_src + 1 + n_rows]
    refs = refs[n_src + 1 + n_rows:]
    outs, vec_out, rows_out = refs[:n_out], refs[n_out], refs[n_out + 1:n_out + 1 + n_rows]
    scratch = refs[n_out + 1 + n_rows:]
    place = Place(dp_size)
    place.greet()
    small = SumAll(place, vec, vec_out, *scratch[13:17])
    sem = scratch[17]
    moves = [SwapBack(place, a, b, sem.at[i, 0], sem.at[i, 1], sem.at[i, 2]) for i, (a, b) in enumerate(zip(rows_in, rows_out))]
    small.begin()
    for move in moves:
        move.start()
    steps = reduce_steps(reduce_units(place, srcs, outs, plan, scratch[:13]))
    for i, step in enumerate(steps):
        for call in step:
            call()
        if i < 4:
            small.advance(i)
    small.finish()
    for move in moves:
        move.wait()


def last_exchange(dp_size, grads, out_shapes, plan, vec, rows, rows_shape):
    n_src, n_out = len(grads), len(out_shapes)
    anywhere = pl.BlockSpec(memory_space=pl.ANY)
    vmem = pl.BlockSpec(memory_space=pltpu.VMEM)
    z = dp_size // 2
    count, width = plan[0][3], plan[0][5]
    n_rows = len(rows)
    return pl.pallas_call(
        functools.partial(last_kernel, dp_size, plan, n_src, n_out, n_rows),
        out_shape=[jax.ShapeDtypeStruct(s, jnp.float32) for s in out_shapes] + [jax.ShapeDtypeStruct(vec.shape, vec.dtype)]
        + [jax.ShapeDtypeStruct(rows_shape, r.dtype) for r in rows],
        in_specs=[anywhere] * n_src + [vmem] + [anywhere] * n_rows,
        out_specs=[anywhere] * n_out + [vmem] + [anywhere] * n_rows,
        scratch_shapes=reduce_scratch(dp_size, len(plan), count, width) + [
            pltpu.VMEM((4, *vec.shape), jnp.float32), pltpu.VMEM((z + 2, *vec.shape), jnp.float32),
            pltpu.SemaphoreType.DMA((z + 2,)), pltpu.SemaphoreType.DMA((z + 2,)), pltpu.SemaphoreType.DMA((n_rows, 3)),
        ],
        compiler_params=pltpu.CompilerParams(collective_id=3, has_side_effects=True, vmem_limit_bytes=60 << 20),
        name="last_exchange",
    )(*grads, vec, *rows)


def halves(width):
    lane = lax.broadcasted_iota(jnp.int32, (1, width), 1)
    return lane


def key_extra(extra_ref, length, core, rows, first_pos):
    block = rows // 4
    row = lax.broadcasted_iota(jnp.int32, (rows, 128), 0)
    lane = lax.broadcasted_iota(jnp.int32, (rows, 128), 1)
    part = row // block
    owner = jnp.where(part < 2, core, 1 - core)
    position = row - part * block + (owner + 2 * lax.rem(part, 2)) * block
    dead = jnp.where(position < length, 0.0, masked_score)
    for parity in range(2):
        base = HEAD_DIM * (1 - parity)
        at = lane - base
        value = jnp.where(at == 0, dead, jnp.where((at > 0) & (at < 4), -1.0, 0.0))
        extra_ref[parity, :, :] = value.astype(jnp.bfloat16)


def split3(value):
    high = value.astype(jnp.bfloat16).astype(jnp.float32)
    rest = value - high
    mid = rest.astype(jnp.bfloat16).astype(jnp.float32)
    return high, mid, rest - mid


def nt(a, b):
    return lax.dot_general(a, b, (((1,), (1,)), ((), ())), preferred_element_type=jnp.float32)


def nn(a, b):
    return jnp.dot(a, b, preferred_element_type=jnp.float32)


def greet_sibling(peer):
    barrier = pltpu.get_barrier_semaphore()
    pl.semaphore_signal(barrier, inc=1, device_id=peer, device_id_type=MESH)
    pl.semaphore_wait(barrier, 1)


def forward_kernel(tile, length_ref, qkv_ref, ctx_ref, lse_ref, other_ref, extra_ref, send, recv):
    seq = lax.axis_index("seq")
    core, side = lax.rem(seq, 2), lax.div(seq, 2)
    peer = (lax.axis_index("dp"), flip(seq, 1))
    rows, width = ctx_ref.shape
    greet_sibling(peer)
    swap = pltpu.make_async_remote_copy(
        src_ref=qkv_ref.at[:, pl.ds(width, 2 * width)], dst_ref=other_ref, send_sem=send, recv_sem=recv,
        device_id=peer, device_id_type=MESH,
    )
    swap.start()
    length = jnp.where(side == 0, length_ref[0], length_ref[1])
    key_extra(extra_ref, length, core, 2 * rows, 0)
    swap.wait()
    lane = lax.broadcasted_iota(jnp.int32, (1, 128), 1)
    lse_ref[...] = jnp.zeros_like(lse_ref)
    slabs = width // 128

    def slab(j, carry):
        at = pl.multiple_of(j * 128, 128)
        cols = lambda base: pl.ds(pl.multiple_of(base + j * 128, 128), 128)
        keys = jnp.concatenate([qkv_ref[:, cols(width)], other_ref[:, cols(0)]], axis=0)
        values = jnp.concatenate([qkv_ref[:, cols(2 * width)], other_ref[:, cols(width)]], axis=0)
        queries = qkv_ref[:, cols(0)]
        outs = []
        stats = []
        for parity in range(2):
            mine = (lane < HEAD_DIM) if parity == 0 else (lane >= HEAD_DIM)
            mark = jnp.where(lane == HEAD_DIM * (1 - parity), 1.0, 0.0).astype(jnp.bfloat16)
            k_h = jnp.where(mine, keys, extra_ref[parity])
            v_h = jnp.where(mine, values, jnp.ones_like(values))
            q_h = jnp.where(mine, queries * jnp.bfloat16(HEAD_DIM ** -0.5), mark)
            pieces, tops = [], []
            for t in range(rows // tile):
                scores = nt(q_h[t * tile:(t + 1) * tile], k_h)
                top = jnp.max(scores, axis=-1, keepdims=True)
                weight = jnp.exp(scores - top).astype(jnp.bfloat16)
                pieces.append(nn(weight, v_h))
                tops.append(top)
            out = jnp.concatenate(pieces, axis=0)
            top = jnp.concatenate(tops, axis=0)
            other = HEAD_DIM * (1 - parity)
            total = out[:, other:other + 1]
            outs.append(out / total)
            stats.append(top + jnp.log(total))
        ctx_ref[:, cols(0)] = jnp.where(lane < HEAD_DIM, outs[0], outs[1]).astype(jnp.bfloat16)
        lse_ref[...] = jnp.where(lane == 2 * j, stats[0], jnp.where(lane == 2 * j + 1, stats[1], lse_ref[...]))
        return carry

    lax.fori_loop(0, slabs, slab, 0)


def attend_forward(lengths, qkv):
    rows, width = qkv.shape[0], qkv.shape[1] // 3
    vmem = pl.BlockSpec(memory_space=pltpu.VMEM)
    return pl.pallas_call(
        functools.partial(forward_kernel, min(256, rows)),
        out_shape=[
            jax.ShapeDtypeStruct((rows, width), jnp.bfloat16),
            jax.ShapeDtypeStruct((rows, 128), jnp.float32),
            jax.ShapeDtypeStruct((rows, 2 * width), jnp.bfloat16),
        ],
        in_specs=[pl.BlockSpec(memory_space=pltpu.SMEM), vmem],
        out_specs=[vmem] * 3,
        scratch_shapes=[pltpu.VMEM((2, 2 * rows, 128), jnp.bfloat16), pltpu.SemaphoreType.DMA, pltpu.SemaphoreType.DMA],
        compiler_params=pltpu.CompilerParams(collective_id=1, has_side_effects=True, vmem_limit_bytes=48 << 20),
        name="attend_forward",
    )(lengths, qkv)


def backward_kernel(block, length_ref, qkv_ref, other_ref, ctx_ref, grad_ref, lse_ref, out_ref,
                    extra_ref, k_ref, v_ref, q_ref, g_ref, kt_ref, dq_ref, dk_ref, dv_ref, got_ref, send, recv):
    seq = lax.axis_index("seq")
    core, side = lax.rem(seq, 2), lax.div(seq, 2)
    peer = (lax.axis_index("dp"), flip(seq, 1))
    rows, width = ctx_ref.shape
    slabs = width // 128
    greet_sibling(peer)
    length = jnp.where(side == 0, length_ref[0], length_ref[1])
    key_extra(extra_ref, length, core, 2 * rows, 0)
    lane = lax.broadcasted_iota(jnp.int32, (1, 128), 1)
    sub = lax.broadcasted_iota(jnp.int32, (128, 1), 0)

    def give(j, which):
        src = (dk_ref if which == 0 else dv_ref).at[j, pl.ds(rows, rows)]
        return pltpu.make_async_remote_copy(
            src_ref=src, dst_ref=got_ref.at[j, which], send_sem=send.at[j, which], recv_sem=recv.at[j, which],
            device_id=peer, device_id_type=MESH,
        )

    def slab(j, carry):
        cols = lambda base: pl.ds(pl.multiple_of(base + j * 128, 128), 128)
        keys = jnp.concatenate([qkv_ref[:, cols(width)], other_ref[:, cols(0)]], axis=0)
        values = jnp.concatenate([qkv_ref[:, cols(2 * width)], other_ref[:, cols(width)]], axis=0)
        queries = qkv_ref[:, cols(0)] * jnp.bfloat16(HEAD_DIM ** -0.5)
        grads = grad_ref[:, cols(0)]
        along = grads.astype(jnp.float32) * ctx_ref[:, cols(0)].astype(jnp.float32)
        lse = lse_ref[...]
        for parity in range(2):
            mine = (lane < HEAD_DIM) if parity == 0 else (lane >= HEAD_DIM)
            at = lane - HEAD_DIM * (1 - parity)
            delta = jnp.sum(jnp.where(mine, along, 0.0), axis=-1, keepdims=True)
            stat = jnp.sum(jnp.where(lane == 2 * j + parity, lse, 0.0), axis=-1, keepdims=True)
            s0, s1, s2 = split3(stat)
            d0, d1, d2 = split3(delta)
            low = jnp.bfloat16
            q_more = jnp.where(at == 0, 1.0, jnp.where(at == 1, s0, jnp.where(at == 2, s1, jnp.where(at == 3, s2, 0.0)))).astype(low)
            g_more = jnp.where(at == 1, d0, jnp.where(at == 2, d1, jnp.where(at == 3, d2, 0.0))).astype(low)
            k_h = jnp.where(mine, keys, extra_ref[parity])
            k_ref[parity] = k_h
            v_ref[parity] = jnp.where(mine, values, extra_ref[parity])
            q_ref[parity] = jnp.where(mine, queries, q_more)
            g_ref[parity] = jnp.where(mine, grads, g_more)
            kt_ref[parity] = jnp.where((sub < HEAD_DIM) if parity == 0 else (sub >= HEAD_DIM), keys.T, jnp.zeros((128, 2 * rows), low))
        dq_ref[...] = jnp.zeros_like(dq_ref)

        def part(b, carry):
            span = pl.ds(pl.multiple_of(b * block, block), block)
            made = []
            for parity in range(2):
                q_h, g_h = q_ref[parity], g_ref[parity]
                prob = jnp.exp(nt(k_ref[parity, span, :], q_h))
                slope = nt(v_ref[parity, span, :], g_h)
                ds = (prob * slope).astype(jnp.bfloat16)
                dv = nn(prob.astype(jnp.bfloat16), g_h)
                dk = nn(ds, q_h)
                dq_ref[...] += nn(kt_ref[parity, :, span], ds)
                made.append((dk, dv))
            dk_ref[j, span, :] = jnp.where(lane < HEAD_DIM, made[0][0], made[1][0])
            dv_ref[j, span, :] = jnp.where(lane < HEAD_DIM, made[0][1], made[1][1])
            return carry

        lax.fori_loop(0, 2 * rows // block, part, 0)
        out_ref[:, cols(0)] = (dq_ref[...].T * (HEAD_DIM ** -0.5)).astype(jnp.bfloat16)
        give(j, 0).start()
        give(j, 1).start()
        return carry

    lax.fori_loop(0, slabs, slab, 0)

    def take(j, carry):
        for which in range(2):
            give(j, which).wait()
            mine = (dk_ref if which == 0 else dv_ref)[j, pl.ds(0, rows), :]
            at = pl.ds(pl.multiple_of((1 + which) * width + j * 128, 128), 128)
            out_ref[:, at] = (mine + got_ref[j, which]).astype(jnp.bfloat16)
        return carry

    lax.fori_loop(0, slabs, take, 0)


def attend_backward(lengths, qkv, other, ctx, grad, lse):
    rows, width = ctx.shape
    slabs = width // 128
    vmem = pl.BlockSpec(memory_space=pltpu.VMEM)
    low = lambda *shape: pltpu.VMEM(shape, jnp.bfloat16)
    full = lambda *shape: pltpu.VMEM(shape, jnp.float32)
    return pl.pallas_call(
        functools.partial(backward_kernel, min(256, rows)),
        out_shape=jax.ShapeDtypeStruct(qkv.shape, jnp.bfloat16),
        in_specs=[pl.BlockSpec(memory_space=pltpu.SMEM)] + [vmem] * 5,
        out_specs=vmem,
        scratch_shapes=[
            low(2, 2 * rows, 128), low(2, 2 * rows, 128), low(2, 2 * rows, 128), low(2, rows, 128), low(2, rows, 128),
            low(2, 128, 2 * rows), full(128, rows), full(slabs, 2 * rows, 128), full(slabs, 2 * rows, 128),
            full(slabs, 2, rows, 128), pltpu.SemaphoreType.DMA((slabs, 2)), pltpu.SemaphoreType.DMA((slabs, 2)),
        ],
        compiler_params=pltpu.CompilerParams(collective_id=2, has_side_effects=True, vmem_limit_bytes=56 << 20),
        name="attend_backward",
    )(lengths, qkv, other, ctx, grad, lse)


class SwapBack:
    def __init__(self, place, src, dst, send, recv, local):
        side, length = place.side, dst.shape[1]
        block = lambda i: src.at[pl.ds(pl.multiple_of(i * length, length), length)]
        self.here = pltpu.make_async_copy(block(side), dst.at[side], local)
        self.there = pltpu.make_async_remote_copy(
            src_ref=block(1 - side), dst_ref=dst.at[side], send_sem=send, recv_sem=recv,
            device_id=(place.dp, flip(place.seq, 2)), device_id_type=MESH,
        )

    def start(self):
        self.here.start()
        self.there.start()

    def wait(self):
        self.here.wait()
        self.there.wait()


def matmul(a, b):
    return jnp.dot(a, b, preferred_element_type=jnp.float32)


def inner_rows(a, b):
    return lax.dot_general(a, b, (((0,), (0,)), ((), ())), preferred_element_type=jnp.float32)


def times_transposed(a, b):
    return lax.dot_general(a, b, (((1,), (1,)), ((), ())), preferred_element_type=jnp.float32)


def swap_rows(rows):
    side = lax.div(lax.axis_index("seq"), 2)
    size = lax.axis_size("seq")
    got = lax.ppermute(lax.dynamic_index_in_dim(rows, 1 - side, 0, False), "seq", [(i, i ^ 2) for i in range(size)])
    kept = lax.dynamic_index_in_dim(rows, side, 0, False)
    first = jnp.where(side == 0, kept, got)
    second = jnp.where(side == 0, got, kept)
    return jnp.concatenate([first, second], axis=0)


def swap_rows_back(rows):
    side = lax.div(lax.axis_index("seq"), 2)
    size = lax.axis_size("seq")
    blocks = rows.reshape(2, rows.shape[0] // 2, rows.shape[1])
    got = lax.ppermute(lax.dynamic_index_in_dim(blocks, 1 - side, 0, False), "seq", [(i, i ^ 2) for i in range(size)])
    kept = lax.dynamic_index_in_dim(blocks, side, 0, False)
    return jnp.stack([jnp.where(side == 0, kept, got), jnp.where(side == 0, got, kept)])


def pack_vectors(narrow, wide):
    rows = jnp.stack([v.astype(jnp.float32) for v in narrow])
    rows = jnp.pad(rows, ((0, 0), (0, 128 - rows.shape[1])))
    more = wide.astype(jnp.float32).reshape(-1, 128)
    both = jnp.concatenate([rows, more], axis=0)
    return jnp.pad(both, ((0, 16 - both.shape[0]), (0, 0)))


def norm_stats(hidden):
    row_mean = jnp.mean(hidden, axis=-1, keepdims=True)
    centred = hidden - row_mean
    row_var = jnp.mean(centred * centred, axis=-1, keepdims=True)
    scale = lax.rsqrt(row_var + eps_norm)
    return centred * scale, scale


def norm_backward(grad, gain, unit, scale):
    e = grad * gain
    first = jnp.mean(e, axis=-1, keepdims=True)
    second = jnp.mean(e * unit, axis=-1, keepdims=True)
    return scale * (e - first - unit * second)


def col_sum(value):
    return jnp.sum(value, axis=0)


def local(
    inputs, lengths, query_weight, key_weight, value_weight, output_weight, up_weight, down_weight,
    query_bias, value_bias, output_bias, up_bias, down_bias, first_gain, first_shift, second_gain, second_shift, cotangent,
):
    dp_size = lax.axis_size("dp")
    groups, length, width = inputs.shape
    shard = query_weight.shape[0]
    fast = dp_size == 8 and shard == 96 and groups == 2
    rows = groups * length
    seq = lax.axis_index("seq")
    core, side = lax.rem(seq, 2), lax.div(seq, 2)
    narrow = [query_bias, value_bias, output_bias, down_bias, first_gain, first_shift, second_gain, second_shift]
    hidden_width = up_weight.shape[1]
    if fast:
        u = shard
        plan = [(i, 0, 0, u, 0, width, width * i) for i in range(3)] + [(3, 1, 0, u, 0, width, 0)]
        plan += [(4, 2, 0, u, width * j, width, width * j) for j in range(hidden_width // width)]
        plan += [(5, 3, u * j, u, 0, width, 0) for j in range(down_weight.shape[0] // u)]
        weights = [query_weight, key_weight, value_weight, output_weight, up_weight, down_weight]
        shapes = [(u, 3 * width), (u, width), (u, hidden_width), (down_weight.shape[0], width)]
        qkv_w, out_w, up_w, down_w, vec, flat_in, flat_cot = first_exchange(
            dp_size, weights, shapes, plan, pack_vectors(narrow, up_bias), (inputs, cotangent)
        )
        qkv_w, out_w = qkv_w.reshape(width, 3 * width), out_w.reshape(width, width)
        up_w, down_w = up_w.reshape(width, hidden_width), down_w.reshape(hidden_width, width)
        vec = vec.reshape(dp_size, 16, 128)
        flat_vec = vec[:, :8, :shard].transpose(1, 0, 2).reshape(8, width)
        bias_up = vec[:, 8:8 + up_bias.shape[0] // 128].reshape(hidden_width)
    else:
        gather = lambda a: lax.all_gather(a, "dp", axis=0, tiled=True)
        qkv_w = gather(jnp.concatenate([query_weight, key_weight, value_weight], axis=1))
        out_w, up_w, down_w = gather(output_weight), gather(up_weight), gather(down_weight)
        flat_vec = jnp.stack([gather(v.astype(jnp.float32)) for v in narrow])
        bias_up = gather(up_bias.astype(jnp.float32))
        flat_in, flat_cot = swap_rows(inputs), swap_rows(cotangent)
    bias_q, bias_v, bias_out, bias_down, gain_1, shift_1, gain_2, shift_2 = [flat_vec[i] for i in range(8)]
    bias_qkv = jnp.concatenate([bias_q, jnp.zeros_like(bias_q), bias_v])

    qkv = (matmul(flat_in, qkv_w) + bias_qkv).astype(jnp.bfloat16)
    context, lse, other = attend_forward(lengths, qkv)
    first_sum = flat_in.astype(jnp.float32) + (matmul(context, out_w) + bias_out)
    unit_1, scale_1 = norm_stats(first_sum)
    first_norm = (unit_1 * gain_1 + shift_1).astype(jnp.bfloat16)
    up_pre = matmul(first_norm, up_w) + bias_up
    below = 0.5 + 0.5 * lax.erf(up_pre * (0.5 ** 0.5))
    hidden_act = (up_pre * below).astype(jnp.bfloat16)
    slope = (below + up_pre * jnp.exp(-0.5 * up_pre * up_pre) * 0.3989422804014327).astype(jnp.bfloat16)
    down_out = matmul(hidden_act, down_w) + bias_down
    second_sum = first_norm.astype(jnp.float32) + down_out
    unit_2, scale_2 = norm_stats(second_sum)
    layer_rows = (unit_2 * gain_2 + shift_2).astype(jnp.bfloat16)

    row = jnp.arange(rows)
    position = lax.rem(row, length) + (core + 2 * lax.div(row, length)) * length
    live = (position < lengths[side]).astype(jnp.float32)
    grad_out = flat_cot.astype(jnp.float32) * live[:, None]
    second_gain_grad, second_shift_grad = col_sum(grad_out * unit_2), col_sum(grad_out)
    second_sum_grad = norm_backward(grad_out, gain_2, unit_2, scale_2)
    down_low = second_sum_grad.astype(jnp.bfloat16)
    low = jnp.bfloat16
    down_w_grad = inner_rows(hidden_act, down_low).astype(low)
    down_bias_grad = col_sum(down_low.astype(jnp.float32))
    up_low = (times_transposed(down_low, down_w) * slope.astype(jnp.float32)).astype(low)
    up_w_grad = inner_rows(first_norm, up_low).astype(low)
    up_bias_grad = col_sum(up_low.astype(jnp.float32))
    norm_grad = second_sum_grad + times_transposed(up_low, up_w)
    first_gain_grad, first_shift_grad = col_sum(norm_grad * unit_1), col_sum(norm_grad)
    first_sum_grad = norm_backward(norm_grad, gain_1, unit_1, scale_1)
    attended_low = first_sum_grad.astype(low)
    out_w_grad = inner_rows(context, attended_low).astype(low)
    out_bias_grad = col_sum(attended_low.astype(jnp.float32))
    context_grad = times_transposed(attended_low, out_w).astype(low)

    qkv_low = attend_backward(lengths, qkv, other, context, context_grad, lse)
    qkv_w_grad = inner_rows(flat_in, qkv_low).astype(low)
    qkv_bias_grad = col_sum(qkv_low.astype(jnp.float32))
    input_rows = (first_sum_grad + times_transposed(qkv_low, qkv_w)).astype(low)

    small = jnp.concatenate([
        jnp.stack([qkv_bias_grad[:width], qkv_bias_grad[2 * width:], out_bias_grad, down_bias_grad, first_gain_grad,
                   first_shift_grad, second_gain_grad, second_shift_grad]),
        up_bias_grad.reshape(-1, width),
    ], axis=0)
    me = lax.axis_index("dp")
    if fast:
        plan = [(3, 5, u * j, u, 0, width, u * j, 0) for j in range(down_weight.shape[0] // u)]
        plan += [(2, 4, 0, u, width * j, width, 0, width * j) for j in range(hidden_width // width)]
        plan += [(1, 3, 0, u, 0, width, 0, 0)] + [(0, i, 0, u, width * i, width, 0, 0) for i in range(3)]
        shapes = [(u, width)] * 4 + [up_weight.shape, down_weight.shape]
        grads = [g.reshape(dp_size // 2, 2, -1, g.shape[1]) for g in (qkv_w_grad, out_w_grad, up_w_grad, down_w_grad)]
        small = jnp.pad(small, ((0, 16 - small.shape[0]), (0, 0)))
        *weight_grads, small, layer_out, input_grad = last_exchange(
            dp_size, grads, shapes, plan, small, (layer_rows, input_rows), (groups, length, width)
        )
    else:
        scatter = lambda a: lax.psum(lax.psum_scatter(a.astype(jnp.float32), "dp", scatter_dimension=0, tiled=True), "seq")
        qkv_g = scatter(qkv_w_grad)
        weight_grads = [qkv_g[:, :width], qkv_g[:, width:2 * width], qkv_g[:, 2 * width:]]
        weight_grads += [scatter(out_w_grad), scatter(up_w_grad), scatter(down_w_grad)]
        small = lax.psum(small, ("dp", "seq"))
        layer_out, input_grad = swap_rows_back(layer_rows), swap_rows_back(input_rows)
    part = query_bias.shape[0]
    mine = lax.dynamic_slice(small, (0, me * part), (8, part))
    up_part = up_bias.shape[0]
    up_mine = lax.dynamic_slice(small[8:8 + hidden_width // width].reshape(hidden_width), (me * up_part,), (up_part,))
    return (layer_out, input_grad, *weight_grads, mine[0], mine[1], mine[2], up_mine, *[mine[i] for i in range(3, 8)])


def solution(mesh):
    rows, matrix, vector = P("dp", "seq", None), P("dp", None), P("dp")
    return jax.shard_map(
        local,
        mesh=mesh,
        in_specs=(rows, vector, *[matrix] * 6, *[vector] * 9, rows),
        out_specs=(rows, rows, *[matrix] * 6, *[vector] * 9),
        check_vma=False,
    )
```

time: 1250 us -> 314 us (0.25)
  waiting for transfers between devices: 784 us -> 0 us
  Pallas kernels: 0 us -> 240 us
  blocking collectives: 149 us -> 0 us
  matrix products: 141 us -> 46.5 us
  local copies, waits for them, and re-layouts: 98.8 us -> 20 us
  other arithmetic: 36 us -> 5.98 us
  between operations: 16.9 us -> 1.05 us
    reduce_scatter x3 -> x0, waiting for transfers between devices: 402 us -> none  [the longest x1 166 us: local(): lax.psum_scatter(up_weight_grad, 'dp', scatter_dimension=0, tiled=True)]
    pallas_call x0 -> x4, Pallas kernels: none -> 240 us  [the longest x1 97.7 us: last_exchange(): pl.pallas_call(functools.partial(last_kernel, dp_size, plan, n_src, n_out...]
    unnamed x16 -> x0, waiting for transfers between devices: 171 us -> none
    all_gather x6 -> x0, waiting for transfers between devices: 140 us -> none  [the longest x1 59.2 us: local(): lax.all_gather(down_weight, 'dp', axis=0, tiled=True)]
    dot_general x46 -> x12, matrix products: 141 us -> 46.5 us  [the longest x4 18.6 us: inner_rows(): lax.dot_general(a, b, (((0,), (0,)), ((), ())), preferred_element_type=jn...]
    unnamed x2 -> x0, blocking collectives: 75.6 us -> none
    all_to_all x1 -> x0, blocking collectives: 40.3 us -> none  [local(): lax.all_to_all(head_grads, 'seq', split_axis=2, concat_axis=3, tiled=True)]
    all_to_all x3 -> x0, waiting for transfers between devices: 39.4 us -> none  [the longest x1 27.9 us: local(): lax.all_to_all(stacked, 'seq', split_axis=3, concat_axis=2, tiled=True)]
  transfers between devices with their start and end apart: 16 -> 0, of which waited for: 13 -> 0; matrix products, arithmetic and copies ran while one was open for 11% -> 0% of each run, Pallas kernels for 0% -> 0%
where the time goes in v1:
time: 314 us; the launch traced here: 313 us
  Pallas kernels  240 us (76%)
  matrix products  46.5 us (15%)
  local copies, waits for them, and re-layouts  20 us (6%)
  other arithmetic  5.98 us (2%)
    pallas_call x1, Pallas kernels, last_exchange(): pl.pallas_call(functools.partial(last_kernel, dp_size, plan, n_src, n_out...  97.7 us
    pallas_call x1, Pallas kernels, first_exchange(): pl.pallas_call(functools.partial(first_kernel, dp_size, plan, n_src, n_ds...  94.6 us
    pallas_call x1, Pallas kernels, attend_backward(): pl.pallas_call(functools.partial(backward_kernel, min(256, rows)), out_sh...  30.5 us
    dot_general x4, matrix products, inner_rows(): lax.dot_general(a, b, (((0,), (0,)), ((), ())), preferred_element_type=jn...  18.6 us
    pallas_call x1, Pallas kernels, attend_forward(): pl.pallas_call(functools.partial(forward_kernel, min(256, rows)), out_sha...  17 us
    dot_general x4, matrix products, times_transposed(): lax.dot_general(a, b, (((1,), (1,)), ((), ())), preferred_element_type=jn...  16.6 us
    unnamed x62, local copies, waits for them, and re-layouts  12.2 us
    dot_general x4, matrix products, matmul(): return jnp.dot(a, b, preferred_element_type=jnp.float32)  11.3 us

profile of v1, /device:TPU:0, one launch (start us, length us, event | category | flops | bytes accessed | tf_op | source)
XLA Modules:
  0.0 313.3 jit_solution(632277722652044245)
XLA Ops:
  0.7 1.2 dynamic_slice.9
  4.7 94.6 %first_exchange.1 = (bf16[4,2,96,2304]{3,2,1,0:T(8,128)(2,1)}, bf16[4,2,96,768]{3,2,1,0:T(8,128)(2,1)}, bf16[4,2,96,3072]{3,2,1,0:T(8,128)(2,1)}, bf16[4,2,384,7...) custom-call(bf16[96,768]{1,0:T(8,128)(2,1)} %refs_0_.1, ...), custom_call_target="tpu_custom_call" | custom-call | tf_op jit(solution)/shard_map/first_exchange/pallas_call | solution.py:253
  101.5 4.3 %fusion.5.qkv_ref = bf16[512,2304]{1,0:T(8,128)(2,1)S(1)} fusion(bf16[512,768]{1,0:T(8,128)(2,1)} %get-tuple-element.36, bf16[768,2304]{1,0:T(8,128)(2,1)} %bitcast.76, f32[2304]{0:T(1024)S(1)} %pad_maximum_fusion), kind=kOutput, calls=%fused_computation.15 | convolution fusion | flops 1814298624 | bytes 6693888 | tf_op jit(solution)/shard_map/dot_general | solution.py:768
  105.8 17.0 %attend_forward.1 = (bf16[512,768]{1,0:T(8,128)(2,1)S(1)}, f32[512,128]{1,0:T(8,128)S(1)}, bf16[512,1536]{1,0:T(8,128)(2,1)S(1)}) custom-call(s32[2]{0:T(128)S(1)} %copy-done.5, bf16[512,2304]{1,0:T(8,128)(2,1)S(1)} %fusion.5.qkv_ref), custom_call_target="tpu_custom_call" | custom-call | tf_op jit(solution)/shard_map/attend_forward/pallas_call | solution.py:631
  122.9 0.9 fusion.17
  124.6 1.5 copy-done.18
  126.1 3.3 %multiply_convert_fusion.1 = (bf16[512,3072]{1,0:T(8,128)(2,1)S(1)}, f32[512,3072]{1,0:T(8,128)S(1)}) fusion(f32[3072]{0:T(1024)S(1)} %add.134, bf16[768,3072]{1,0:T(8,128)(2,1)S(1)} %bitcast.70, f32[512,768]{1,0:T(8,128)S(1)} %get-tuple-element.87, f32[768]{0:T(1024)S(1)} %add.131, f32[768]{0:T(1024)S(1)} %mul.161, f32[512]{0:T(512)S(1)} %add_rsqrt_fusion.1, ...), kind=kOutput, calls=%fused_computation.8 | convolution fusion | flops 2427322368 | bytes 15751168 | tf_op jit(solution)/shard_map/dot_general | solution.py:768
  129.5 2.8 fusion.18
  133.4 1.9 multiply_reduce_fusion
  136.0 5.0 %convert_reduce_fusion = (f32[3072]{0:T(1024)S(1)}, bf16[512,3072]{1,0:T(8,128)(2,1)S(1)}) fusion(f32[512,3072]{1,0:T(8,128)S(1)} %get-tuple-element.89, f32[3072]{0:T(1024)S(1)} %add.134, bf16[3072,768]{1,0:T(8,128)(2,1)S(1)} %bitcast.75, f32[512,768]{1,0:T(8,128)S(1)} %get-tuple-element.72), kind=kOutput, calls=%fused_computation.6 | convolution fusion | flops 2439902208 | bytes 15753216 | tf_op jit(solution)/shard_map/dot_general | solution.py:776
  141.0 4.2 %multiply_reduce_fusion.1 = (f32[768]{0:T(1024)S(1)}, f32[512]{0:T(512)S(1)}, f32[512]{0:T(512)S(1)}, f32[768]{0:T(1024)S(1)}, f32[512,768]{1,0:T(8,128)}) fusion(f32[512,768]{1,0:T(8,128)S(1)} %get-tuple-element.87, f32[512]{0:T(512)S(1)} %add_rsqrt_fusion.1, f32[512]{0:T(512)S(1)} %broadcast_multiply_fusion.5, f32[768]{0:T(1024)S(1)} %mul.161, ...), kind=kOutput, calls=%fused_computation.19 | convolution fusion | flops 2419848704 | bytes 12600320 | tf_op jit(solution)/shard_map/dot_general | solution.py:776
  145.2 6.8 %convolution_convert_fusion = bf16[3072,768]{1,0:T(8,128)(2,1)} fusion(bf16[512,3072]{1,0:T(8,128)(2,1)} %copy-done.22, f32[512,768]{1,0:T(8,128)S(1)} %get-tuple-element.72), kind=kOutput, calls=%fused_computation.10 | convolution fusion | flops 2418671616 | bytes 9437184 | tf_op jit(solution)/shard_map/dot_general | solution.py:772
  152.5 1.4 copy-done.24
  153.9 4.9 %convolution_convert_fusion.1 = bf16[768,3072]{1,0:T(8,128)(2,1)} fusion(bf16[512,3072]{1,0:T(8,128)(2,1)S(1)} %copy-done.24, f32[512,768]{1,0:T(8,128)S(1)} %get-tuple-element.87, f32[768]{0:T(1024)S(1)} %add.131, f32[768]{0:T(1024)S(1)} %mul.161, f32[512]{0:T(512)S(1)} %add_rsqrt_fusion.1, f32[512]{0:T(512)S(1)} %broadcast_multiply_fusion.5), kind=kOutput, calls=%fused_computation.11 | convolution fusion | flops 2420244480 | bytes 9447424 | tf_op jit(solution)/shard_map/dot_general | solution.py:772
  158.8 1.7 convolution_convert_fusion.4.grad_ref
  160.5 30.5 %attend_backward.1 = bf16[512,2304]{1,0:T(8,128)(2,1)} custom-call(s32[2]{0:T(128)} %length_ref.3, bf16[512,2304]{1,0:T(8,128)(2,1)} %copy-done, bf16[512,1536]{1,0:T(8,128)(2,1)} %copy-done.3, bf16[512,768]{1,0:T(8,128)(2,1)} %copy-done.1, bf16[512,768]{1,0:T(8,128)(2,1)} %convolution_convert_fusion.4.grad_ref, f32[512,128]{1,0:T(8,128)} %copy-done.4), custom_call_target="tpu_custom_call" | custom-call | tf_op jit(solution)/shard_map/attend_backward/pallas_call | solution.py:733
  191.0 5.8 %add_convert_fusion.refs_6_ = bf16[512,768]{1,0:T(8,128)(2,1)} fusion(f32[512,768]{1,0:T(8,128)S(1)} %get-tuple-element.74, bf16[512,2304]{1,0:T(8,128)(2,1)} %attend_backward.1, bf16[768,2304]{1,0:T(8,128)(2,1)} %bitcast.77), kind=kOutput, calls=%fused_computation.16 | convolution fusion | flops 1812725760 | bytes 8257536 | tf_op jit(solution)/shard_map/dot_general | solution.py:776
  197.9 5.1 %convolution_convert_fusion.2 = bf16[768,2304]{1,0:T(8,128)(2,1)} fusion(bf16[512,768]{1,0:T(8,128)(2,1)} %get-tuple-element.36, bf16[512,2304]{1,0:T(8,128)(2,1)S(1)} %copy-done.6), kind=kOutput, calls=%fused_computation.12 | convolution fusion | flops 1813708800 | bytes 6684672 | tf_op jit(solution)/shard_map/dot_general | solution.py:772
  203.0 1.8 convolution_convert_fusion.3
  204.9 97.7 %last_exchange.1 = (f32[96,768]{1,0:T(8,128)}, f32[96,768]{1,0:T(8,128)}, f32[96,768]{1,0:T(8,128)}, f32[96,768]{1,0:T(8,128)}, f32[96,3072]{1,0:T(8,128)}, /*in...) custom-call(bf16[4,2,96,2304]{3,2,1,0:T(8,128)(2,1)} %bitcast.58, ...), custom_call_target="tpu_custom_call" | custom-call | tf_op jit(solution)/shard_map/last_exchange/pallas_call | solution.py:520
  305.3 2.1 copy.43
  307.5 0.9 copy.44
  311.2 1.0 copy.49
  312.2 1.0 copy.50
  (104 shorter events, 14.9 us)
Async XLA Ops:
  101.5 4.3 %copy-start.5 = (s32[2]{0:T(128)S(1)}, s32[2]{0:T(128)}, u32[]{:S(2)}) copy-start(s32[2]{0:T(128)} %length_ref.3) | copy-start | bytes 28
  105.8 18.0 %copy-start = (bf16[512,2304]{1,0:T(8,128)(2,1)}, bf16[512,2304]{1,0:T(8,128)(2,1)S(1)}, u32[]{:S(2)}) copy-start(bf16[512,2304]{1,0:T(8,128)(2,1)S(1)} %fusion.5.qkv_ref) | copy-start | bytes 7077892
  105.8 17.0 %copy-start.19 = (bf16[4,2,96,768]{3,2,1,0:T(8,128)(2,1)S(1)}, bf16[4,2,96,768]{3,2,1,0:T(8,128)(2,1)}, u32[]{:S(2)}) copy-start(bf16[4,2,96,768]{3,2,1,0:T(8,128)(2,1)} %get-tuple-element.41) | copy-start | bytes 3538948
  105.8 17.0 %copy-start.21 = (bf16[512,768]{1,0:T(8,128)(2,1)S(1)}, bf16[512,768]{1,0:T(8,128)(2,1)}, u32[]{:S(2)}) copy-start(bf16[512,768]{1,0:T(8,128)(2,1)} %get-tuple-element.36) | copy-start | bytes 2359300
  122.8 1.5 copy-start.4
  122.9 3.2 %copy-start.18 = (bf16[4,2,96,3072]{3,2,1,0:T(8,128)(2,1)S(1)}, bf16[4,2,96,3072]{3,2,1,0:T(8,128)(2,1)}, u32[]{:S(2)}) copy-start(bf16[4,2,96,3072]{3,2,1,0:T(8,128)(2,1)} %get-tuple-element.42) | copy-start | bytes 14155780
  124.3 5.1 %slice-start = ((s8[4718592]{0:T(1024)(128)(4,1)}), s8[4194304]{0:T(1024)(128)(4,1)S(1)}, s32[]{:S(2)}) async-start(s8[4718592]{0:T(1024)(128)(4,1)} %bitcast.72), calls=%async_computation | async-start | bytes 8388608
  126.1 3.3 %slice-start.1 = ((s8[4718592]{0:T(1024)(128)(4,1)}), s8[524288]{0:T(1024)(128)(4,1)S(1)}, s32[]{:S(2)}) async-start(s8[4718592]{0:T(1024)(128)(4,1)} %bitcast.72), calls=%async_computation.1 | async-start | bytes 1048576
  129.4 2.9 copy-start.22
  141.0 4.2 %copy-start.23 = (bf16[512,3072]{1,0:T(8,128)(2,1)}, bf16[512,3072]{1,0:T(8,128)(2,1)S(1)}, u32[]{:S(2)}) copy-start(bf16[512,3072]{1,0:T(8,128)(2,1)S(1)} %get-tuple-element.94) | copy-start | bytes 9437188
  145.2 6.8 %copy-start.10 = (f32[512,768]{1,0:T(8,128)S(1)}, f32[512,768]{1,0:T(8,128)}, u32[]{:S(2)}) copy-start(f32[512,768]{1,0:T(8,128)} %get-tuple-element.92) | copy-start | bytes 4718596
  152.0 1.9 copy-start.24
  153.9 37.1 %copy-start.7 = (f32[512,768]{1,0:T(8,128)}, f32[512,768]{1,0:T(8,128)S(1)}, u32[]{:S(2)}) copy-start(f32[512,768]{1,0:T(8,128)S(1)} %get-tuple-element.74) | copy-start | bytes 4718596
  153.9 4.9 %copy-start.20 = (bf16[4,2,96,768]{3,2,1,0:T(8,128)(2,1)S(1)}, bf16[4,2,96,768]{3,2,1,0:T(8,128)(2,1)}, u32[]{:S(2)}) copy-start(bf16[4,2,96,768]{3,2,1,0:T(8,128)(2,1)} %get-tuple-element.41) | copy-start | bytes 3538948
  191.0 5.8 %copy-start.6 = (bf16[512,2304]{1,0:T(8,128)(2,1)S(1)}, bf16[512,2304]{1,0:T(8,128)(2,1)}, u32[]{:S(2)}) copy-start(bf16[512,2304]{1,0:T(8,128)(2,1)} %attend_backward.1) | copy-start | bytes 7077892
  197.9 5.1 %copy-start.2 = (bf16[512,768]{1,0:T(8,128)(2,1)S(1)}, bf16[512,768]{1,0:T(8,128)(2,1)}, u32[]{:S(2)}) copy-start(bf16[512,768]{1,0:T(8,128)(2,1)} %copy-done.1) | copy-start | bytes 2359300
  197.9 5.1 %copy-start.8 = (f32[512,768]{1,0:T(8,128)S(1)}, f32[512,768]{1,0:T(8,128)}, u32[]{:S(2)}) copy-start(f32[512,768]{1,0:T(8,128)} %copy-done.7) | copy-start | bytes 4718596
  302.5 4.9 %copy-start.13 = (bf16[2,256,768]{2,1,0:T(8,128)(2,1)S(1)}, bf16[2,256,768]{2,1,0:T(8,128)(2,1)}, u32[]{:S(2)}) copy-start(bf16[2,256,768]{2,1,0:T(8,128)(2,1)} %get-tuple-element.115) | copy-start | bytes 2359300
  305.3 3.0 copy-start.17
  305.3 3.7 %copy-start.16 = (f32[96,768]{1,0:T(8,128)S(1)}, f32[96,768]{1,0:T(8,128)}, u32[]{:S(2)}) copy-start(f32[96,768]{1,0:T(8,128)} %get-tuple-element.117) | copy-start | bytes 884740
  307.5 2.3 copy-start.15
  307.5 3.0 copy-start.14
  308.4 2.9 copy-start.12
  310.5 1.7 copy-start.11
  (3 other events, 3.5 us)
